TPU v7x, 32 devices: a whole 2x2x4 slice. The times are simulated.
32 devices in a mesh: dp: 8 (over y, x, core), tensor: 4 (over z).
Axes of the slice: x: 2, y: 2, z: 4, core: 2. Of those that a mesh axis runs over, the one named last changes fastest.
Arguments:
- gate_pre: bfloat16 [3072, 14336], P('dp', 'tensor'), may hold values from -6 to 6
- up_pre: bfloat16 [3072, 14336], P('dp', 'tensor'), may hold values from -6 to 6
- out_grad: bfloat16 [3072, 4096], P('dp'), may hold values from -6 to 6
- old_weight: float32 [14336, 4096], P(('dp', 'tensor')), may hold values from -0.046875 to 0.046875
- old_first: float32 [14336, 4096], P(('dp', 'tensor')), may hold values from -8 to 8
- old_second: float32 [14336, 4096], P(('dp', 'tensor')), may hold values from 1 to 1000
Outputs:
- new_weight: float32 [14336, 4096], P('tensor', 'dp')
- new_first: float32 [14336, 4096], P('tensor', 'dp')
- new_second: float32 [14336, 4096], P('tensor', 'dp')
- grad_gate: bfloat16 [3072, 14336], P('dp', 'tensor')
- grad_up: bfloat16 [3072, 14336], P('dp', 'tensor')
All inputs are finite; a program needn't handle non-finite values.
Results may differ from a plain program's by a relative error of at most 0.0051.
Values may be sent and summed in bfloat16 or wider, within the bound.
No kernel may reach another device: no remote copies, remote signals or barrier semaphores. Data moves between devices by JAX's collectives and lax.ppermute only.
A program may use at most 256 MiB of HBM per device.

v0:
```python
import jax
import jax.numpy as jnp
from jax import lax
from jax.sharding import PartitionSpec as P

beta_one = 0.9
beta_two = 0.95
learn_rate = 0.0003
decay_rate = 0.1
epsilon = 1e-08
step_count = 1001


def adamw(weight, first, second, grad):
    first_new = beta_one * first + (1.0 - beta_one) * grad
    second_new = beta_two * second + (1.0 - beta_two) * grad * grad
    first_hat = first_new / (1.0 - beta_one**step_count)
    second_hat = second_new / (1.0 - beta_two**step_count)
    weight_new = weight - learn_rate * (
        first_hat / (jnp.sqrt(second_hat) + epsilon) + decay_rate * weight
    )
    return (weight_new, first_new, second_new)


def retile(moved, dp_count, tensor_count):
    row_total = moved.shape[0]
    col_count = moved.shape[1]
    block_rows = row_total // dp_count
    shaped = moved.reshape(tensor_count, dp_count // tensor_count, block_rows, col_count)
    return jnp.transpose(shaped, (1, 0, 2, 3)).reshape(row_total, col_count)


def body(gate_pre, up_pre, out_grad, old_weight, old_first, old_second):
    dp_count = lax.axis_size("dp")
    tensor_count = lax.axis_size("tensor")
    moved = (
        lax.all_to_all(
            lax.all_to_all(old_weight, "dp", split_axis=1, concat_axis=0, tiled=True),
            "tensor",
            split_axis=0,
            concat_axis=0,
            tiled=True,
        ),
        lax.all_to_all(
            lax.all_to_all(old_first, "dp", split_axis=1, concat_axis=0, tiled=True),
            "tensor",
            split_axis=0,
            concat_axis=0,
            tiled=True,
        ),
        lax.all_to_all(
            lax.all_to_all(old_second, "dp", split_axis=1, concat_axis=0, tiled=True),
            "tensor",
            split_axis=0,
            concat_axis=0,
            tiled=True,
        ),
    )
    weight_tile = retile(moved[0], dp_count, tensor_count)
    first_tile = retile(moved[1], dp_count, tensor_count)
    second_tile = retile(moved[2], dp_count, tensor_count)
    gate_f = gate_pre.astype(jnp.float32)
    up_f = up_pre.astype(jnp.float32)
    sig = jax.nn.sigmoid(gate_f)
    hidden = (gate_f * sig * up_f).astype(jnp.bfloat16)
    weight_half = weight_tile.astype(jnp.bfloat16)
    hidden_grad = lax.dot_general(
        out_grad,
        lax.all_gather(weight_half, "dp", axis=1, tiled=True),
        (((1,), (1,)), ((), ())),
        preferred_element_type=jnp.float32,
    )
    grad_gate = (hidden_grad * up_f * sig * (1.0 + gate_f * (1.0 - sig))).astype(jnp.bfloat16)
    grad_up = (hidden_grad * gate_f * sig).astype(jnp.bfloat16)
    partial_grad = lax.dot_general(
        hidden, out_grad, (((0,), (0,)), ((), ())), preferred_element_type=jnp.float32
    )
    rounded = lax.optimization_barrier(partial_grad.astype(jnp.bfloat16)).astype(jnp.float32)
    weight_grad = lax.psum_scatter(rounded, "dp", scatter_dimension=1, tiled=True)
    new_weight, new_first, new_second = adamw(weight_tile, first_tile, second_tile, weight_grad)
    return (new_weight, new_first, new_second, grad_gate, grad_up)


def solution(mesh):
    placed = (
        P("dp", "tensor"),
        P("dp", "tensor"),
        P("dp", None),
        P(("dp", "tensor"), None),
        P(("dp", "tensor"), None),
        P(("dp", "tensor"), None),
    )
    return jax.shard_map(
        body,
        mesh=mesh,
        in_specs=placed,
        out_specs=(
            P("tensor", "dp"),
            P("tensor", "dp"),
            P("tensor", "dp"),
            P("dp", "tensor"),
            P("dp", "tensor"),
        ),
        check_vma=False,
    )
```

profile of v0, /device:TPU:0, one launch (start us, length us, event | category | flops | bytes accessed | tf_op | source)
XLA Modules:
  0.0 962.9 jit_solution(4845986395762285044)
XLA Ops:
  7.2 0.0 copy-start
  7.2 0.0 all-gather.2.cloned.1.call-start
  7.2 4.4 copy.34
  11.7 87.7 %all_to_all.75 = f32[448,8,512]{2,0,1:T(8,128)S(1)} all-to-all(f32[448,8,512]{2,0,1:T(8,128)S(1)} %bitcast.56), channel_id=1, replica_groups=mesh['dp'=8,'tensor'=4] {'dp'}, dimensions={1} | all-to-all | bytes 14680064 | tf_op jit(solution)/shard_map/all_to_all | solution.py:38
  99.4 164.7 %all_to_all.76 = f32[4,896,512]{2,1,0:T(8,128)S(1)} all-to-all(f32[4,896,512]{2,1,0:T(8,128)S(1)} %bitcast.52), channel_id=1, replica_groups=mesh['dp'=8,'tensor'=4] {'tensor'}, dimensions={0} | all-to-all | bytes 14680064 | tf_op jit(solution)/shard_map/all_to_all | solution.py:37
  264.1 0.8 copy.21
  264.9 0.0 copy-start.1
  264.9 2.9 copy-done.1
  267.8 2.3 bitcast_convert_fusion
  270.1 0.0 all-gather.2.cloned.1.call-update
  270.1 0.0 reduce-scatter.2.cloned.1.call-start
  270.2 0.0 copy-done
  270.2 23.1 %convolution_convert_fusion = bf16[3584,4096]{1,0:T(8,128)(2,1)} fusion(bf16[384,4096]{1,0:T(8,128)(2,1)S(1)} %copy-done, bf16[384,3584]{1,0:T(8,128)(2,1)} %param.7, bf16[384,3584]{1,0:T(8,128)(2,1)} %param.6), kind=kOutput, calls=%fused_computation | convolution fusion | flops 11299979264 | bytes 38010880 | tf_op jit(solution)/shard_map/dot_general | solution.py:75
  293.3 28.2 %convert_element_type.28 = f32[3584,4096]{1,0:T(8,128)} convert(bf16[3584,4096]{1,0:T(8,128)(2,1)} %convolution_convert_fusion) | non-fusion elementwise | flops 14680064 | bytes 88080384 | tf_op jit(solution)/shard_map/convert_element_type | solution.py:78
  321.5 0.0 reduce-scatter.2.cloned.1.call-update
  321.6 8.4 copy.33
  330.0 4.9 all-to-all-start.2
  334.9 7.6 copy.32
  342.6 145.2 %all-to-all-done.2 = f32[448,8,512]{2,0,1:T(8,128)} async-done(((f32[448,8,512]{2,0,1:T(8,128)}), f32[448,8,512]{2,0,1:T(8,128)}, u32[]{:S(2)}, u32[]{:S(2)}) %all-to-all-start.2) | async-done | bytes 7340064 | tf_op jit(solution)/shard_map/all_to_all | solution.py:45
  487.8 88.4 %all_to_all.77 = f32[448,8,512]{2,0,1:T(8,128)} all-to-all(f32[448,8,512]{2,0,1:T(8,128)} %bitcast.51), channel_id=1, replica_groups=mesh['dp'=8,'tensor'=4] {'dp'}, dimensions={1} | all-to-all | bytes 14680064 | tf_op jit(solution)/shard_map/all_to_all | solution.py:52
  576.2 167.5 %all_to_all.78 = f32[4,896,512]{2,1,0:T(8,128)} all-to-all(f32[4,896,512]{2,1,0:T(8,128)} %bitcast.6), channel_id=1, replica_groups=mesh['dp'=8,'tensor'=4] {'tensor'}, dimensions={0} | all-to-all | bytes 14680064 | tf_op jit(solution)/shard_map/all_to_all | solution.py:44
  743.7 5.6 all-to-all-start.5
  749.3 4.4 broadcast_multiply_fusion.1
  753.7 3.8 copy.23
  757.5 151.2 %all-to-all-done.5 = f32[4,896,512]{2,1,0:T(8,128)} async-done(((f32[4,896,512]{2,1,0:T(8,128)}), f32[4,896,512]{2,1,0:T(8,128)}, u32[]{:S(2)}, u32[]{:S(2)}) %all-to-all-start.5) | async-done | bytes 7340064 | tf_op jit(solution)/shard_map/all_to_all | solution.py:51
  908.7 4.0 broadcast_multiply_fusion
  912.7 3.8 copy.25
  916.6 0.0 all-gather.2.cloned.1.call-done
  916.6 20.2 %fusion.12 = (bf16[384,3584]{1,0:T(8,128)(2,1)}, bf16[384,3584]{1,0:T(8,128)(2,1)}) fusion(bf16[384,3584]{1,0:T(8,128)(2,1)} %param.6, bf16[384,3584]{1,0:T(8,128)(2,1)} %param.7, bf16[384,4096]{1,0:T(8,128)(2,1)S(1)} %copy-done, bf16[3584,4096]{1,0:T(8,128)(2,1)} %all-gather.2.cloned.1.call-done), kind=kOutput, calls=%fused_computation.27 | convolution fusion | flops 11294932992 | bytes 43515904 | tf_op jit(solution)/shard_map/dot_general | solution.py:67
  936.8 0.0 reduce-scatter.2.cloned.1.call-done
  936.8 19.3 %bitcast_subtract_fusion = (f32[3584,512]{1,0:T(8,128)}, f32[3584,512]{1,0:T(8,128)}, f32[3584,512]{1,0:T(8,128)}) fusion(f32[2,4,448,512]{3,2,1,0:T(8,128)} %copy-done.1, f32[3584,512]{1,0:T(8,128)} %reduce-scatter.2.cloned.1.call-done, f32[2,4,448,512]{3,2,1,0:T(8,128)} %copy.25, f32[2,4,448,512]{3,2,1,0:T(8,128)} %copy.23), kind=kLoop, calls=%fused_computation.12 | loop fusion | flops 20185088 | bytes 51380224 | tf_op jit(solution)/shard_map/sub | solution.py:19
Async XLA Ops:
  7.2 263.0 %copy-start = (bf16[384,4096]{1,0:T(8,128)(2,1)S(1)}, bf16[384,4096]{1,0:T(8,128)(2,1)}, u32[]{:S(2)}) copy-start(bf16[384,4096]{1,0:T(8,128)(2,1)} %param.8) | copy-start | bytes 9437188
  7.2 909.4 %all-gather.2.cloned.1.call-start = ((), (), s32[]{:S(2)}) async-start(), calls=%async_computation.8 | async-start | bytes 33030144 | tf_op jit(solution)/shard_map/all_gather | solution.py:69
  264.9 2.9 copy-start.1
  270.1 666.6 %reduce-scatter.2.cloned.1.call-start = ((), (), s32[]{:S(2)}) async-start(), calls=%async_computation.7 | async-start | bytes 66060288 | tf_op jit(solution)/shard_map/reduce_scatter | solution.py:79
  330.0 157.8 %all-to-all-start.2 = ((f32[448,8,512]{2,0,1:T(8,128)}), f32[448,8,512]{2,0,1:T(8,128)}, u32[]{:S(2)}, u32[]{:S(2)}) async-start(f32[448,8,512]{2,0,1:T(8,128)} %bitcast.50), calls=%async_computation.2 | async-start | bytes 14680064 | tf_op jit(solution)/shard_map/all_to_all | solution.py:45
  743.7 165.0 %all-to-all-start.5 = ((f32[4,896,512]{2,1,0:T(8,128)}), f32[4,896,512]{2,1,0:T(8,128)}, u32[]{:S(2)}, u32[]{:S(2)}) async-start(f32[4,896,512]{2,1,0:T(8,128)} %bitcast.49), calls=%async_computation.6 | async-start | bytes 14680064 | tf_op jit(solution)/shard_map/all_to_all | solution.py:51
Sparse Core Ops, SparseCore 0:
  270.3 216.0 all-gather.1
  489.9 333.7 reduce-scatter.1
where the time goes:
time: 964 us; the launch traced here: 963 us
  blocking collectives  508 us (53%)
  waiting for transfers between devices  296 us (31%)
  other arithmetic  58.2 us (6%)
  matrix products  43.3 us (4%)
  local copies, waits for them, and re-layouts  31.9 us (3%)
  between operations  14.1 us (1%)
  starting transfers between devices  10.6 us (1%)
    all_to_all x1, blocking collectives, body(): lax.all_to_all(lax.all_to_all(old_first, 'dp', split_axis=1, concat_axis=...  168 us
    all_to_all x1, blocking collectives, body(): lax.all_to_all(lax.all_to_all(old_weight, 'dp', split_axis=1, concat_axis...  165 us
    all_to_all x1, waiting for transfers between devices, body(): lax.all_to_all(lax.all_to_all(old_second, 'dp', split_axis=1, concat_axis...  151 us
    all_to_all x1, waiting for transfers between devices, body(): lax.all_to_all(old_first, 'dp', split_axis=1, concat_axis=0, tiled=True)  145 us
    all_to_all x1, blocking collectives, body(): lax.all_to_all(old_second, 'dp', split_axis=1, concat_axis=0, tiled=True)  88.4 us
    all_to_all x1, blocking collectives, body(): lax.all_to_all(old_weight, 'dp', split_axis=1, concat_axis=0, tiled=True)  87.7 us
    convert_element_type x1, other arithmetic, body(): lax.optimization_barrier(partial_grad.astype(jnp.bfloat16))  28.2 us
    dot_general x1, matrix products, body(): lax.dot_general(hidden, out_grad, (((0,), (0,)), ((), ())), preferred_ele...  23.1 us
  transfers between devices with their start and end apart: 4, of which 2 were waited for; matrix products, arithmetic and copies ran while one was open for 11% of the time, Pallas kernels for 0%

commit v1 on v0

v1 whole, which is shorter than its diff:
```python
import functools

import jax
import jax.numpy as jnp
from jax import lax
from jax.experimental import pallas as pl
from jax.experimental.pallas import tpu as pltpu
from jax.sharding import PartitionSpec as P


beta_one = 0.9
beta_two = 0.95
learn_rate = 0.0003
decay_rate = 0.1
epsilon = 1e-08
step_count = 1001


def adamw(weight, first, second, grad):
    first_new = beta_one * first + (1.0 - beta_one) * grad
    second_new = beta_two * second + (1.0 - beta_two) * grad * grad
    first_hat = first_new * (1.0 / (1.0 - beta_one**step_count))
    second_hat = second_new * (1.0 / (1.0 - beta_two**step_count))
    weight_new = weight - learn_rate * (
        first_hat / (second_hat * lax.rsqrt(second_hat) + epsilon) + decay_rate * weight
    )
    return (weight_new, first_new, second_new)


def rows_of(tokens, width, block):
    return pl.BlockSpec((tokens, width), lambda i: (block, 0))


def hidden_gradient(grads, weights, step):
    chips = len(weights)
    flat = [pair for group in grads for pair in group]
    rows, width = weights[0].shape
    tokens = flat[0][0].shape[0] // flat[0][2]

    def kernel(*refs):
        left, right, outs = refs[: 4 * chips], refs[4 * chips : 5 * chips], refs[5 * chips :]
        for n in range(4):
            total = None
            for at in range(chips):
                term = lax.dot_general(
                    left[n * chips + at][...],
                    right[at][...],
                    (((1,), (1,)), ((), ())),
                    preferred_element_type=jnp.float32,
                )
                total = term if total is None else total + term
            if n < 2:
                outs[n][...] = total
            else:
                at = (n - 2) * tokens
                outs[2][at : at + tokens] = total.astype(jnp.bfloat16)

    return pl.pallas_call(
        kernel,
        grid=(rows // step,),
        in_specs=[rows_of(tokens, width, block) for x, block, n in flat]
        + [pl.BlockSpec((step, width), lambda i: (i, 0))] * chips,
        out_specs=[pl.BlockSpec((tokens, step), lambda i: (0, i))] * 2
        + [pl.BlockSpec((2 * tokens, step), lambda i: (0, i))],
        out_shape=[jax.ShapeDtypeStruct((tokens, rows), jnp.float32)] * 2
        + [jax.ShapeDtypeStruct((2 * tokens, rows), jnp.bfloat16)],
        cost_estimate=pl.CostEstimate(
            flops=8 * chips * tokens * rows * width,
            bytes_accessed=8 * chips * tokens * width + 12 * tokens * rows,
            transcendentals=0,
        ),
        name="hidden_gradient",
    )(*[x for x, block, n in flat], *weights)


def weight_gradient(hidden, grads, step):
    chips = len(grads[0])
    flat = [pair for group in grads for pair in group]
    tokens = hidden[0].shape[0] // 2
    rows = hidden[0].shape[1]
    width = flat[0][0].shape[1]

    def kernel(*refs):
        held, right, outs = refs[:2], refs[2 : 2 + 4 * chips], refs[2 + 4 * chips :]
        for at in range(chips):
            total = None
            for n in range(4):
                low = n % 2 * tokens
                term = lax.dot_general(
                    held[n // 2][low : low + tokens],
                    right[n * chips + at][...],
                    (((0,), (0,)), ((), ())),
                    preferred_element_type=jnp.float32,
                )
                total = term if total is None else total + term
            outs[at][...] = total.astype(outs[at].dtype)

    return pl.pallas_call(
        kernel,
        grid=(rows // step,),
        in_specs=[pl.BlockSpec((2 * tokens, step), lambda i: (0, i))] * 2
        + [rows_of(tokens, width, block) for x, block, n in flat],
        out_specs=[pl.BlockSpec((step, width), lambda i: (i, 0))] * chips,
        out_shape=[
            jax.ShapeDtypeStruct((rows, width), jnp.bfloat16 if at else jnp.float32)
            for at in range(chips)
        ],
        cost_estimate=pl.CostEstimate(
            flops=8 * chips * tokens * rows * width,
            bytes_accessed=8 * chips * tokens * width + 8 * tokens * rows + 6 * rows * width,
            transcendentals=0,
        ),
        name="weight_gradient",
    )(*hidden, *[x for x, block, n in flat])


def update_half(place, side, weights, firsts, seconds, grad, so_far):
    block_rows = weights[0].shape[1]
    rows_all, cols = grad.shape
    planes = rows_all // block_rows
    cuts = 2 if block_rows % 32 == 0 else 1
    rows = block_rows // cuts
    arrays = len(weights)

    def kernel(place_ref, grad_ref, *refs):
        outs = refs[-3:]
        for n in range(arrays):

            @pl.when((pl.program_id(0) == n) | (arrays == 1))
            def _(held=refs[n : 3 * arrays : arrays]):
                new = adamw(*[ref[0].astype(jnp.float32) for ref in held], grad_ref[...])
                for out, value in zip(outs, new):
                    out[...] = value

    def row(s, i, place_ref):
        return (s ^ place_ref[1]) * cuts + i

    def grad_index(s, i, place_ref):
        return (row(s, i, place_ref), 0)

    def out_index(s, i, place_ref):
        return ((side ^ place_ref[0]) * planes * cuts + row(s, i, place_ref), 0)

    def held_index(n, s, i, place_ref):
        if arrays == 1:
            return (s, i, 0)
        return (0, jnp.clip((s - n) * cuts + i, 0, cuts - 1), place_ref[0])

    shape = jax.ShapeDtypeStruct((2 * rows_all, cols), jnp.float32)
    return pl.pallas_call(
        kernel,
        grid_spec=pltpu.PrefetchScalarGridSpec(
            num_scalar_prefetch=1,
            grid=(planes, cuts),
            in_specs=[pl.BlockSpec((rows, cols), grad_index)]
            + [
                pl.BlockSpec((1, rows, cols), functools.partial(held_index, at))
                for _ in range(3)
                for at in range(arrays)
            ]
            + [pl.BlockSpec(memory_space=pl.ANY)] * len(so_far),
            out_specs=[pl.BlockSpec((rows, cols), out_index)] * 3,
        ),
        out_shape=[shape] * 3,
        input_output_aliases={2 + 3 * arrays + n: n for n in range(len(so_far))},
        cost_estimate=pl.CostEstimate(
            flops=20 * rows_all * cols,
            bytes_accessed=22 * rows_all * cols,
            transcendentals=2 * rows_all * cols,
        ),
        name="update_half",
    )(place, grad, *weights, *firsts, *seconds, *so_far)


def body(gate_pre, up_pre, out_grad, old_weight, old_first, old_second):
    dp_count = lax.axis_size("dp")
    planes = lax.axis_size("tensor")
    chips = dp_count // 2
    dp_index = lax.axis_index("dp")
    chip, core = dp_index // 2, dp_index % 2
    plane = lax.axis_index("tensor")
    place = jnp.stack([core, plane]).astype(jnp.int32)
    block_rows, width = old_weight.shape
    cols = width // dp_count
    tokens, hidden_cols = gate_pre.shape
    half = hidden_cols // 2

    def to_chip(x, step):
        return lax.ppermute(x, "dp", [(d, d ^ (2 * step)) for d in range(dp_count)])

    def to_plane(x, step):
        return lax.ppermute(x, "tensor", [(t, t ^ step) for t in range(planes)])

    def to_partner(x):
        return lax.ppermute(x, "dp", [(d, d ^ 1) for d in range(dp_count)])

    def pick(items, index):
        chosen = items[0]
        for i in range(1, len(items)):
            chosen = jnp.where(index == i, items[i], chosen)
        return chosen

    def chip_columns(x, step):
        return lax.dynamic_slice_in_dim(x, (chip ^ step) * 2 * cols, 2 * cols, 1)

    def exchange(x):
        cut = [chip_columns(x, s).astype(jnp.bfloat16)[None] for s in range(chips)]
        held = [cut[0]] + [to_chip(cut[s], s) for s in range(1, chips)]
        sent = [pick(held, plane ^ s ^ chip) for s in range(planes)]
        return [sent[0]] + [to_plane(sent[s], s) for s in range(1, planes)]

    weight_got = exchange(old_weight)
    first_got = exchange(old_first)
    second_got = exchange(old_second)

    bits = (1, 2)
    groups = [[s for s in range(chips) if not s & bit] for bit in bits]
    step = next(n for n in (256, 128, 64) if half % n == 0 and half > n)
    blocks = half // step
    sizes = [(blocks - blocks // 2) * step, blocks // 2 * step]
    lows = [0, sizes[0]]

    pieces = [chip_columns(out_grad, s) for s in range(chips)]
    near = [
        to_chip(jnp.concatenate([pieces[s ^ bit] for s in group], 0), bit)
        for bit, group in zip(bits, groups)
    ]
    own_grad = jnp.concatenate(pieces, 0)
    own_part = to_partner(own_grad)
    near_part = [to_partner(x) for x in near]
    grads = [
        [[(x, s, chips) for s in group] for x in (own_grad, own_part)]
        + [[(x, n, len(group)) for n in range(len(group))] for x in (near[p], near_part[p])]
        for p, group in enumerate(groups)
    ]

    gate_f = gate_pre.astype(jnp.float32)
    up_f = up_pre.astype(jnp.float32)
    hidden = (gate_f * jax.nn.sigmoid(gate_f) * up_f).astype(jnp.bfloat16)
    hidden_own = lax.dynamic_slice_in_dim(hidden, core * half, half, 1)
    hidden_other = lax.dynamic_slice_in_dim(hidden, (1 - core) * half, half, 1)
    hidden_part = to_partner(hidden_other)
    hidden_held = []
    for p, bit in enumerate(bits):
        at = slice(lows[p], lows[p] + sizes[p])
        own = jnp.concatenate([hidden_own[:, at], hidden_part[:, at]], 0)
        hidden_held.append([own, to_chip(own, bit)])

    weight_grads = []
    for p, group in enumerate(groups):
        terms = weight_gradient(hidden_held[p], grads[p], step)
        came = [to_chip(terms[n], s) for n, s in enumerate(group) if n]
        weight_grads.append([terms[0]] + came)

    weight_rows = jnp.zeros((planes * block_rows, 2 * cols), jnp.bfloat16)
    for s in range(planes):
        weight_rows = lax.dynamic_update_slice(
            weight_rows, weight_got[s][0], ((plane ^ s) * block_rows, 0)
        )
    own_sum, partner_sum = [], []
    for p, (bit, group) in enumerate(zip(bits, groups)):
        own = weight_rows[lows[p] : lows[p] + sizes[p]]
        held = [own] + [to_chip(own, s) for s in group[1:]]
        kept, kept_part, sent = hidden_gradient(grads[p], held, step)
        came = to_chip(sent, bit)
        own_sum.append(kept + came[:tokens].astype(jnp.float32))
        total = kept_part + came[tokens:].astype(jnp.float32)
        partner_sum.append(to_partner(total))

    def columns_of(x, side):
        return lax.dynamic_slice_in_dim(x, side * cols, cols, x.ndim - 1)

    def other_columns(held):
        return jnp.concatenate([columns_of(x, 1 - core) for x in held], 0)

    weight_other = other_columns(weight_got)
    first_other = other_columns(first_got)
    second_other = other_columns(second_got)
    sums = [
        [sum(columns_of(x, side).astype(jnp.float32) for x in terms) for terms in weight_grads]
        for side in (core, 1 - core)
    ]
    grad_own, grad_other = (jnp.concatenate(x, 0) for x in sums)
    weight_came = to_partner(weight_other)
    first_came = to_partner(first_other)
    grad_came = to_partner(grad_other)
    second_came = to_partner(second_other)
    updated = update_half(place, 0, weight_got, first_got, second_got, grad_own, ())
    updated = update_half(place, 1, [weight_came], [first_came], [second_came], grad_came, updated)

    gate_late, up_late = lax.optimization_barrier((gate_pre, up_pre))
    own, other = jnp.concatenate(own_sum, 1), jnp.concatenate(partner_sum, 1)
    hidden_grad = jnp.where(
        core == 0, jnp.concatenate([own, other], 1), jnp.concatenate([other, own], 1)
    )
    gate_f = gate_late.astype(jnp.float32)
    up_f = up_late.astype(jnp.float32)
    sig = jax.nn.sigmoid(gate_f)
    grad_gate = (hidden_grad * up_f * sig * (1.0 + gate_f * (1.0 - sig))).astype(jnp.bfloat16)
    grad_up = (hidden_grad * gate_f * sig).astype(jnp.bfloat16)
    return (*updated, grad_gate, grad_up)


def solution(mesh):
    placed = (
        P("dp", "tensor"),
        P("dp", "tensor"),
        P("dp", None),
        P(("dp", "tensor"), None),
        P(("dp", "tensor"), None),
        P(("dp", "tensor"), None),
    )

    return jax.shard_map(
        body,
        mesh=mesh,
        in_specs=placed,
        out_specs=(
            P("tensor", "dp"),
            P("tensor", "dp"),
            P("tensor", "dp"),
            P("dp", "tensor"),
            P("dp", "tensor"),
        ),
        check_vma=False,
    )
```

time: 964 us -> 468 us (0.49)
  blocking collectives: 508 us -> 0 us
  waiting for transfers between devices: 296 us -> 222 us
  starting transfers between devices: 10.6 us -> 78.9 us
  Pallas kernels: 0 us -> 67.7 us
  matrix products: 43.3 us -> 0 us
  between operations: 14.1 us -> 1.21 us
    all_to_all x4 -> x0, blocking collectives: 508 us -> none  [the longest x1 168 us: body(): lax.all_to_all(lax.all_to_all(old_first, 'dp', split_axis=1, concat_axis=...]
    all_to_all x2 -> x0, waiting for transfers between devices: 296 us -> none  [the longest x1 151 us: body(): lax.all_to_all(lax.all_to_all(old_second, 'dp', split_axis=1, concat_axis...]
    ppermute x0 -> x38, waiting for transfers between devices: none -> 222 us  [the longest x19 138 us: to_chip(): return lax.ppermute(x, 'dp', [(d, d ^ 2 * step) for d in range(dp_count)])]
    ppermute x0 -> x38, starting transfers between devices: none -> 78.9 us  [the longest x9 48.7 us: to_plane(): return lax.ppermute(x, 'tensor', [(t, t ^ step) for t in range(planes)])]
    pallas_call x0 -> x6, Pallas kernels: none -> 67.7 us  [the longest x2 24.3 us: weight_gradient(): pl.pallas_call(kernel, grid=(rows // step,), in_specs=[pl.BlockSpec((2 *...]
    dot_general x2 -> x0, matrix products: 43.3 us -> none  [the longest x1 23.1 us: body(): lax.dot_general(hidden, out_grad, (((0,), (0,)), ((), ())), preferred_ele...]
    all_to_all x3 -> x0, local copies, waits for them, and re-layouts: 20.5 us -> none  [the longest x1 8.41 us: body(): lax.all_to_all(old_first, 'dp', split_axis=1, concat_axis=0, tiled=True)]
    sub x1 -> x0, other arithmetic: 19.3 us -> none  [adamw(): weight - learn_rate * (first_hat / (jnp.sqrt(second_hat) + epsilon) + dec...]
  transfers between devices with their start and end apart: 4 -> 38, of which waited for: 2 -> 13; matrix products, arithmetic and copies ran while one was open for 11% -> 19% of each run, Pallas kernels for 0% -> 12%
where the time goes in v1:
time: 468 us; the launch traced here: 467 us
  waiting for transfers between devices  222 us (47%)
  starting transfers between devices  78.9 us (17%)
  Pallas kernels  67.7 us (14%)
  other arithmetic  56.3 us (12%)
  local copies, waits for them, and re-layouts  41 us (9%)
    ppermute x19, waiting for transfers between devices, to_chip(): return lax.ppermute(x, 'dp', [(d, d ^ 2 * step) for d in range(dp_count)])  138 us
    ppermute x9, waiting for transfers between devices, to_plane(): return lax.ppermute(x, 'tensor', [(t, t ^ step) for t in range(planes)])  83.9 us
    ppermute x9, starting transfers between devices, to_plane(): return lax.ppermute(x, 'tensor', [(t, t ^ step) for t in range(planes)])  48.7 us
    ppermute x19, starting transfers between devices, to_chip(): return lax.ppermute(x, 'dp', [(d, d ^ 2 * step) for d in range(dp_count)])  28.9 us
    pallas_call x2, Pallas kernels, weight_gradient(): pl.pallas_call(kernel, grid=(rows // step,), in_specs=[pl.BlockSpec((2 *...  24.3 us
    pallas_call x2, Pallas kernels, update_half(): pl.pallas_call(kernel, grid_spec=pltpu.PrefetchScalarGridSpec(num_scalar_...  22.3 us
    pallas_call x2, Pallas kernels, hidden_gradient(): pl.pallas_call(kernel, grid=(rows // step,), in_specs=[rows_of(tokens, wi...  21 us
    select_n x5, other arithmetic, pick(): chosen = jnp.where(index == i, items[i], chosen)  17.4 us
  transfers between devices with their start and end apart: 38, of which 13 were waited for; matrix products, arithmetic and copies ran while one was open for 19% of the time, Pallas kernels for 12%

profile of v1, /device:TPU:0, one launch (start us, length us, event | category | flops | bytes accessed | tf_op | source)
XLA Modules:
  0.0 467.4 jit_solution(17016964314602913982)
XLA Ops:
  0.7 4.3 fusion.15
  5.0 3.0 collective-permute-start.13
  9.4 4.5 fusion.19
  19.0 5.3 %fusion.23 = (bf16[1,448,1024]{2,1,0:T(8,128)(2,1)}, bf16[1,448,1024]{2,1,0:T(8,128)(2,1)}, bf16[1,448,1024]{2,1,0:T(8,128)(2,1)}) fusion(f32[448,4096]{1,0:T(8,128)} %param.11, s32[]{:T(128)S(6)} %select_n.260, s32[]{:T(128)S(6)} %select_n.261, s32[]{:T(128)S(6)} %select_n.262), kind=kLoop, calls=%fused_computation.59 | loop fusion | bytes 5505036 | tf_op jit(solution)/shard_map/broadcast_in_dim | solution.py:207
  29.4 3.0 collective-permute-start.18
  32.4 18.7 %collective-permute-done.12 = bf16[1,448,1024]{2,1,0:T(8,128)(2,1)} collective-permute-done((bf16[1,448,1024]{2,1,0:T(8,128)(2,1)}, bf16[1,448,1024]{2,1,0:T(8,128)(2,1)}, u32[]{:S(2)}, u32[]{:S(2)}) %collective-permute-start.12) | collective-permute-done | bytes 917536 | tf_op jit(solution)/shard_map/ppermute | solution.py:189
  54.4 14.4 %collective-permute-done.20 = bf16[1,448,1024]{2,1,0:T(8,128)(2,1)} collective-permute-done((bf16[1,448,1024]{2,1,0:T(8,128)(2,1)}, bf16[1,448,1024]{2,1,0:T(8,128)(2,1)}, u32[]{:S(2)}, u32[]{:S(2)}) %collective-permute-start.20) | collective-permute-done | bytes 917536 | tf_op jit(solution)/shard_map/ppermute | solution.py:189
  68.8 20.6 %collective-permute-done.19 = bf16[1,448,1024]{2,1,0:T(8,128)(2,1)} collective-permute-done((bf16[1,448,1024]{2,1,0:T(8,128)(2,1)}, bf16[1,448,1024]{2,1,0:T(8,128)(2,1)}, u32[]{:S(2)}, u32[]{:S(2)}) %collective-permute-start.19) | collective-permute-done | bytes 917536 | tf_op jit(solution)/shard_map/ppermute | solution.py:189
  92.4 3.2 bitcast_dynamic-update-slice_fusion.3
  95.6 5.0 %select_select_fusion.10 = (bf16[1,448,1024]{2,1,0:T(8,128)(2,1)}, bf16[1,448,1024]{2,1,0:T(8,128)(2,1)}, bf16[1,448,1024]{2,1,0:T(8,128)(2,1)}) fusion(bf16[1,448,1024]{2,1,0:T(8,128)(2,1)} %collective-permute-done.11, bf16[1,448,1024]{2,1,0:T(8,128)(2,1)} %collective-permute-done.12, bf16[1,448,1024]{2,1,0:T(8,128)(2,1)} %collective-permute-done.13, ...), kind=kLoop, calls=%fused_computation.75 | loop fusion | flops 4128768 | bytes 6422537 | tf_op jit(solution)/shard_map/jit(_where)/select_n | solution.py:200
  102.2 5.9 %collective-permute-done.27 = bf16[1,448,1024]{2,1,0:T(8,128)(2,1)} collective-permute-done((bf16[1,448,1024]{2,1,0:T(8,128)(2,1)}, bf16[1,448,1024]{2,1,0:T(8,128)(2,1)}, u32[]{:S(2)}, u32[]{:S(2)}) %collective-permute-start.27) | collective-permute-done | bytes 917536 | tf_op jit(solution)/shard_map/ppermute | solution.py:189
  108.2 4.1 collective-permute-start.16
  117.9 23.1 %collective-permute-done.3.refs_6_.refs_7_.refs_4_.refs_5_ = bf16[768,1024]{1,0:T(8,128)(2,1)} collective-permute-done((bf16[768,1024]{1,0:T(8,128)(2,1)}, bf16[768,1024]{1,0:T(8,128)(2,1)}, u32[]{:S(2)}, u32[]{:S(2)}) %collective-permute-start.3) | collective-permute-done | bytes 1572896 | tf_op jit(solution)/shard_map/ppermute | solution.py:189
  141.0 2.8 collective-permute-start.15
  151.2 3.7 select_select_fusion.6
  156.2 32.9 %collective-permute-done.15.refs_2_ = bf16[1,448,1024]{2,1,0:T(8,128)(2,1)S(1)} collective-permute-done((bf16[1,448,1024]{2,1,0:T(8,128)(2,1)S(1)}, bf16[1,448,1024]{2,1,0:T(8,128)(2,1)S(1)}, u32[]{:S(2)}, u32[]{:S(2)}) %collective-permute-start.15) | collective-permute-done | bytes 917536 | tf_op jit(solution)/shard_map/ppermute | solution.py:192
  193.9 3.1 select_select_fusion.3
  199.3 4.6 collective-permute-done.1.refs_1_
  205.2 3.3 select_select_fusion.2
  213.0 13.3 %weight_gradient.2 = (f32[1024,1024]{1,0:T(8,128)}, bf16[1024,1024]{1,0:T(8,128)(2,1)}) custom-call(bf16[768,1024]{1,0:T(8,128)(2,1)} %copy-done.30, bf16[768,1024]{1,0:T(8,128)(2,1)} %copy-done.42, bf16[1536,1024]{1,0:T(8,128)(2,1)} %copy-done, bf16[1536,1024]{1,0:T(8,128)(2,1)} %copy-done, ...), custom_call_target="tpu_custom_call" | custom-call | flops 6442450944 | bytes 15728640 | tf_op jit(solution)/shard_map/weight_gradient/pallas_call | solution.py:98
  226.4 39.4 %collective-permute-done.6.refs_1_ = bf16[768,768]{1,0:T(8,128)(2,1)} collective-permute-done((bf16[768,768]{1,0:T(8,128)(2,1)}, bf16[768,768]{1,0:T(8,128)(2,1)}, u32[]{:S(2)}, u32[]{:S(2)}) %collective-permute-start.6) | collective-permute-done | bytes 1179680 | tf_op jit(solution)/shard_map/ppermute | solution.py:189
  269.8 11.0 %weight_gradient.3 = (f32[768,1024]{1,0:T(8,128)}, bf16[768,1024]{1,0:T(8,128)(2,1)}) custom-call(bf16[768,768]{1,0:T(8,128)(2,1)} %pad_maximum_fusion.9.refs_0_, bf16[768,768]{1,0:T(8,128)(2,1)} %collective-permute-done.6.refs_1_, bf16[1536,1024]{1,0:T(8,128)(2,1)} %copy-done, bf16[1536,1024]{1,0:T(8,128)(2,1)} %copy-done, ...), custom_call_target="tpu_custom_call" | custom-call | flops 4831838208 | bytes 13369344 | tf_op jit(solution)/shard_map/weight_gradient/pallas_call | solution.py:98
  283.1 11.4 %hidden_gradient.2 = (f32[384,1024]{1,0:T(8,128)}, f32[384,1024]{1,0:T(8,128)}, bf16[768,1024]{1,0:T(8,128)(2,1)}) custom-call(bf16[1536,1024]{1,0:T(8,128)(2,1)} %copy-done, bf16[1536,1024]{1,0:T(8,128)(2,1)} %copy-done, bf16[1536,1024]{1,0:T(8,128)(2,1)} %collective-permute-done.2.refs_4_.refs_5_.refs_2_.refs_3_, ...), custom_call_target="tpu_custom_call" | custom-call | flops 6442450944 | bytes 11010048 | tf_op jit(solution)/shard_map/hidden_gradient/pallas_call | solution.py:58
  299.8 34.5 %collective-permute-start.28 = (bf16[1,448,1024]{2,1,0:T(8,128)(2,1)}, bf16[1,448,1024]{2,1,0:T(8,128)(2,1)}, u32[]{:S(2)}, u32[]{:S(2)}) collective-permute-start(bf16[1,448,1024]{2,1,0:T(8,128)(2,1)} %get-tuple-element.63), channel_id=1, source_target_pairs={{0,1},{1,0},{2,3},{3,2},{4,5},{5,4},{6,7},{7,6},{8,9},{9,8},{10,11... | collective-permute-start | bytes 2752520 | tf_op jit(solution)/shard_map/ppermute | solution.py:192
  334.3 9.6 %hidden_gradient.3 = (f32[384,768]{1,0:T(8,128)}, f32[384,768]{1,0:T(8,128)}, bf16[768,768]{1,0:T(8,128)(2,1)}) custom-call(bf16[1536,1024]{1,0:T(8,128)(2,1)} %copy-done, bf16[1536,1024]{1,0:T(8,128)(2,1)} %copy-done, bf16[1536,1024]{1,0:T(8,128)(2,1)} %collective-permute-done.2.refs_4_.refs_5_.refs_2_.refs_3_, ...), custom_call_target="tpu_custom_call" | custom-call | flops 4831838208 | bytes 9830400 | tf_op jit(solution)/shard_map/hidden_gradient/pallas_call | solution.py:58
  358.5 4.0 convert_add_fusion.2
  362.4 10.0 %collective-permute-done.35 = bf16[768,768]{1,0:T(8,128)(2,1)S(1)} collective-permute-done((bf16[768,768]{1,0:T(8,128)(2,1)}, bf16[768,768]{1,0:T(8,128)(2,1)S(1)}, u32[]{:S(2)}, u32[]{:S(2)}) %collective-permute-start.35) | collective-permute-done | bytes 1179680 | tf_op jit(solution)/shard_map/ppermute | solution.py:189
  373.9 11.2 %collective-permute-done.28.refs_9_ = bf16[1,448,1024]{2,1,0:T(8,128)(2,1)} collective-permute-done((bf16[1,448,1024]{2,1,0:T(8,128)(2,1)}, bf16[1,448,1024]{2,1,0:T(8,128)(2,1)}, u32[]{:S(2)}, u32[]{:S(2)}) %collective-permute-start.28) | collective-permute-done | bytes 917536 | tf_op jit(solution)/shard_map/ppermute | solution.py:192
  388.3 37.8 %collective-permute-done.29.refs_10_ = bf16[1,448,1024]{2,1,0:T(8,128)(2,1)S(1)} collective-permute-done((bf16[1,448,1024]{2,1,0:T(8,128)(2,1)S(1)}, bf16[1,448,1024]{2,1,0:T(8,128)(2,1)S(1)}, u32[]{:S(2)}, u32[]{:S(2)}) %collective-permute-start.29) | collective-permute-done | bytes 917536 | tf_op jit(solution)/shard_map/ppermute | solution.py:192
  434.6 11.1 %update_half.2 = (f32[3584,512]{1,0:T(8,128)}, f32[3584,512]{1,0:T(8,128)}, f32[3584,512]{1,0:T(8,128)}) custom-call(s32[2]{0:T(128)} %pad_add_fusion.place_ref, f32[1792,512]{1,0:T(8,128)} %pad_maximum_fusion.1.grad_ref, bf16[1,448,1024]{2,1,0:T(8,128)(2,1)} %get-tuple-element.42.refs_0_, bf16[1,448,1024]{2,1,0:T(8,128)(2,1)} %collective-permute-done.14.refs_1_, ...), custom_call_target="tpu_custom_call" | custom-call | flops 18350080 | bytes 20185088 | tf_op jit(solution)/shard_map/update_half/pallas_call | solution.py:150
  445.7 10.4 %fusion.11 = (bf16[384,3584]{1,0:T(8,128)(2,1)}, bf16[384,3584]{1,0:T(8,128)(2,1)}) fusion(bf16[384,3584]{1,0:T(8,128)(2,1)} %param.6, f32[384,768]{1,0:T(8,128)} %get-tuple-element.79, f32[384,1024]{1,0:T(8,128)} %get-tuple-element.77, f32[384,768]{1,0:T(8,128)} %copy-done.35, f32[384,1024]{1,0:T(8,128)} %collective-permute-done.36, pred[]{:T(512)S(6)} %eq.77, ...), kind=kLoop, calls=%fused_computation.16 | loop fusion | flops 30277632 | bytes 16515073 | tf_op jit(solution)/shard_map/convert_element_type | solution.py:300
  456.1 11.2 %update_half.3 = (f32[3584,512]{1,0:T(8,128)}, f32[3584,512]{1,0:T(8,128)}, f32[3584,512]{1,0:T(8,128)}) custom-call(s32[2]{0:T(128)} %pad_add_fusion.place_ref, f32[1792,512]{1,0:T(8,128)} %collective-permute-done.10.grad_ref, bf16[4,448,512]{2,1,0:T(8,128)(2,1)} %collective-permute-done.17.refs_0_, ...), custom_call_target="tpu_custom_call", output_to_operand_aliasing={{0}: (5, {}), {1}: (6, {}), {2}: (7, {})} | custom-call | flops 18350080 | bytes 20185088 | tf_op jit(solution)/shard_map/update_half/pallas_call | solution.py:150
  (185 shorter events, 85.5 us)
Async XLA Ops:
  7.9 43.2 %collective-permute-start.12 = (bf16[1,448,1024]{2,1,0:T(8,128)(2,1)}, bf16[1,448,1024]{2,1,0:T(8,128)(2,1)}, u32[]{:S(2)}, u32[]{:S(2)}) collective-permute-start(bf16[1,448,1024]{2,1,0:T(8,128)(2,1)} %get-tuple-element.57), channel_id=1, source_target_pairs={{0,16},{4,20},{8,24},{12,28},{16,0},{20,4},{24,8},{28,12},{1,17},{... | collective-permute-start | bytes 2752520 | tf_op jit(solution)/shard_map/ppermute | solution.py:189
  9.4 41.7 %collective-permute-start.11 = (bf16[1,448,1024]{2,1,0:T(8,128)(2,1)}, bf16[1,448,1024]{2,1,0:T(8,128)(2,1)}, u32[]{:S(2)}, u32[]{:S(2)}) collective-permute-start(bf16[1,448,1024]{2,1,0:T(8,128)(2,1)} %get-tuple-element.58), channel_id=1, source_target_pairs={{0,24},{4,28},{8,16},{12,20},{16,8},{20,12},{24,0},{28,4},{1,25},{... | collective-permute-start | bytes 2752520 | tf_op jit(solution)/shard_map/ppermute | solution.py:189
  13.9 54.9 %collective-permute-start.20 = (bf16[1,448,1024]{2,1,0:T(8,128)(2,1)}, bf16[1,448,1024]{2,1,0:T(8,128)(2,1)}, u32[]{:S(2)}, u32[]{:S(2)}) collective-permute-start(bf16[1,448,1024]{2,1,0:T(8,128)(2,1)} %get-tuple-element.53), channel_id=1, source_target_pairs={{0,8},{4,12},{8,0},{12,4},{16,24},{20,28},{24,16},{28,20},{1,9},{5... | collective-permute-start | bytes 2752520 | tf_op jit(solution)/shard_map/ppermute | solution.py:189
  15.9 73.5 %collective-permute-start.19 = (bf16[1,448,1024]{2,1,0:T(8,128)(2,1)}, bf16[1,448,1024]{2,1,0:T(8,128)(2,1)}, u32[]{:S(2)}, u32[]{:S(2)}) collective-permute-start(bf16[1,448,1024]{2,1,0:T(8,128)(2,1)} %get-tuple-element.54), channel_id=1, source_target_pairs={{0,16},{4,20},{8,24},{12,28},{16,0},{20,4},{24,8},{28,12},{1,17},{... | collective-permute-start | bytes 2752520 | tf_op jit(solution)/shard_map/ppermute | solution.py:189
  29.4 71.2 %collective-permute-start.18 = (bf16[1,448,1024]{2,1,0:T(8,128)(2,1)}, bf16[1,448,1024]{2,1,0:T(8,128)(2,1)}, u32[]{:S(2)}, u32[]{:S(2)}) collective-permute-start(bf16[1,448,1024]{2,1,0:T(8,128)(2,1)} %get-tuple-element.55), channel_id=1, source_target_pairs={{0,24},{4,28},{8,16},{12,20},{16,8},{20,12},{24,0},{28,4},{1,25},{... | collective-permute-start | bytes 2752520 | tf_op jit(solution)/shard_map/ppermute | solution.py:189
  51.1 57.0 %collective-permute-start.27 = (bf16[1,448,1024]{2,1,0:T(8,128)(2,1)}, bf16[1,448,1024]{2,1,0:T(8,128)(2,1)}, u32[]{:S(2)}, u32[]{:S(2)}) collective-permute-start(bf16[1,448,1024]{2,1,0:T(8,128)(2,1)} %get-tuple-element.50), channel_id=1, source_target_pairs={{0,8},{4,12},{8,0},{12,4},{16,24},{20,28},{24,16},{28,20},{1,9},{5... | collective-permute-start | bytes 2752520 | tf_op jit(solution)/shard_map/ppermute | solution.py:189
  51.1 89.9 %collective-permute-start.3 = (bf16[768,1024]{1,0:T(8,128)(2,1)}, bf16[768,1024]{1,0:T(8,128)(2,1)}, u32[]{:S(2)}, u32[]{:S(2)}) collective-permute-start(bf16[768,1024]{1,0:T(8,128)(2,1)} %get-tuple-element.80), channel_id=1, source_target_pairs={{0,8},{4,12},{8,0},{12,4},{16,24},{20,28},{24,16},{28,20},{1,9},{5... | collective-permute-start | bytes 4718600 | tf_op jit(solution)/shard_map/ppermute | solution.py:189
  68.8 47.5 %collective-permute-start = (bf16[384,1792]{1,0:T(8,128)(2,1)}, bf16[384,1792]{1,0:T(8,128)(2,1)}, u32[]{:S(2)}, u32[]{:S(2)}) collective-permute-start(bf16[384,1792]{1,0:T(8,128)(2,1)} %constant_dynamic-slice_fusion.17), channel_id=1, source_target_pairs={{0,4},{4,0},{8,12},{12,8},{16,20},{20,16},{24,28},{28,24},{1,5},{5... | collective-permute-start | bytes 4128776 | tf_op jit(solution)/shard_map/ppermute | solution.py:195
  100.6 47.2 %collective-permute-start.14 = (bf16[1,448,1024]{2,1,0:T(8,128)(2,1)}, bf16[1,448,1024]{2,1,0:T(8,128)(2,1)}, u32[]{:S(2)}, u32[]{:S(2)}) collective-permute-start(bf16[1,448,1024]{2,1,0:T(8,128)(2,1)} %get-tuple-element.69), channel_id=1, source_target_pairs={{0,1},{1,0},{2,3},{3,2},{4,5},{5,4},{6,7},{7,6},{8,9},{9,8},{10,11... | collective-permute-start | bytes 2752520 | tf_op jit(solution)/shard_map/ppermute | solution.py:192
  108.2 42.4 %collective-permute-start.16 = (bf16[1,448,1024]{2,1,0:T(8,128)(2,1)}, bf16[1,448,1024]{2,1,0:T(8,128)(2,1)}, u32[]{:S(2)}, u32[]{:S(2)}) collective-permute-start(bf16[1,448,1024]{2,1,0:T(8,128)(2,1)} %get-tuple-element.70), channel_id=1, source_target_pairs={{0,3},{1,2},{2,1},{3,0},{4,7},{5,6},{6,5},{7,4},{8,11},{9,10},{10,... | collective-permute-start | bytes 2752520 | tf_op jit(solution)/shard_map/ppermute | solution.py:192
  112.9 98.5 %collective-permute-start.2 = (bf16[1536,1024]{1,0:T(8,128)(2,1)S(1)}, bf16[1536,1024]{1,0:T(8,128)(2,1)}, u32[]{:S(2)}, u32[]{:S(2)}) collective-permute-start(bf16[1536,1024]{1,0:T(8,128)(2,1)S(1)} %pad_maximum_fusion.2.refs_2_.refs_3_.refs_0_.refs_1_), channel_id=1, source_target_pairs={{0,4},{4,0},{8,12},{12,8},{16,20},{20,16},{24,28},{28,24},{1,5},{5... | collective-permute-start | bytes 9437192 | tf_op jit(solution)/shard_map/ppermute | solution.py:195
  116.3 75.8 %collective-permute-start.7 = (bf16[768,1024]{1,0:T(8,128)(2,1)S(1)}, bf16[768,1024]{1,0:T(8,128)(2,1)}, u32[]{:S(2)}, u32[]{:S(2)}) collective-permute-start(bf16[768,1024]{1,0:T(8,128)(2,1)S(1)} %copy-done.31), channel_id=1, source_target_pairs={{0,16},{4,20},{8,24},{12,28},{16,0},{20,4},{24,8},{28,12},{1,17},{... | collective-permute-start | bytes 4718600 | tf_op jit(solution)/shard_map/ppermute | solution.py:189
  141.0 48.0 %collective-permute-start.15 = (bf16[1,448,1024]{2,1,0:T(8,128)(2,1)S(1)}, bf16[1,448,1024]{2,1,0:T(8,128)(2,1)S(1)}, u32[]{:S(2)}, u32[]{:S(2)}) collective-permute-start(bf16[1,448,1024]{2,1,0:T(8,128)(2,1)S(1)} %copy-done.40), channel_id=1, source_target_pairs={{0,2},{1,3},{2,0},{3,1},{4,6},{5,7},{6,4},{7,5},{8,10},{9,11},{10,... | collective-permute-start | bytes 2752520 | tf_op jit(solution)/shard_map/ppermute | solution.py:192
  147.9 44.5 %collective-permute-start.25 = (bf16[1,448,1024]{2,1,0:T(8,128)(2,1)S(1)}, bf16[1,448,1024]{2,1,0:T(8,128)(2,1)S(1)}, u32[]{:S(2)}, u32[]{:S(2)}) collective-permute-start(bf16[1,448,1024]{2,1,0:T(8,128)(2,1)S(1)} %copy-done.38), channel_id=1, source_target_pairs={{0,24},{4,28},{8,16},{12,20},{16,8},{20,12},{24,0},{28,4},{1,25},{... | collective-permute-start | bytes 2752520 | tf_op jit(solution)/shard_map/ppermute | solution.py:189
  150.6 53.2 %collective-permute-start.1 = (bf16[768,1024]{1,0:T(8,128)(2,1)S(1)}, bf16[768,1024]{1,0:T(8,128)(2,1)S(1)}, u32[]{:S(2)}, u32[]{:S(2)}) collective-permute-start(bf16[768,1024]{1,0:T(8,128)(2,1)S(1)} %pad_maximum_fusion.8.refs_0_), channel_id=1, source_target_pairs={{0,8},{4,12},{8,0},{12,4},{16,24},{20,28},{24,16},{28,20},{1,9},{5... | collective-permute-start | bytes 4718600 | tf_op jit(solution)/shard_map/ppermute | solution.py:189
  192.1 76.1 %collective-permute-start.8 = (bf16[768,1024]{1,0:T(8,128)(2,1)}, bf16[768,1024]{1,0:T(8,128)(2,1)}, u32[]{:S(2)}, u32[]{:S(2)}) collective-permute-start(bf16[768,1024]{1,0:T(8,128)(2,1)} %collective-permute-done.7.refs_6_.refs_7_.refs_4_.refs_5_), channel_id=1, source_target_pairs={{0,4},{4,0},{8,12},{12,8},{16,20},{20,16},{24,28},{28,24},{1,5},{5... | collective-permute-start | bytes 4718600 | tf_op jit(solution)/shard_map/ppermute | solution.py:195
  192.4 90.7 %collective-permute-start.32 = (bf16[1024,1024]{1,0:T(8,128)(2,1)}, bf16[1024,1024]{1,0:T(8,128)(2,1)}, u32[]{:S(2)}, u32[]{:S(2)}) collective-permute-start(bf16[1024,1024]{1,0:T(8,128)(2,1)} %slice.42.refs_8_), channel_id=1, source_target_pairs={{0,16},{4,20},{8,24},{12,28},{16,0},{20,4},{24,8},{28,12},{1,17},{... | collective-permute-start | bytes 6291464 | tf_op jit(solution)/shard_map/ppermute | solution.py:189
  203.8 61.9 %collective-permute-start.6 = (bf16[768,768]{1,0:T(8,128)(2,1)}, bf16[768,768]{1,0:T(8,128)(2,1)}, u32[]{:S(2)}, u32[]{:S(2)}) collective-permute-start(bf16[768,768]{1,0:T(8,128)(2,1)} %pad_maximum_fusion.9.refs_0_), channel_id=1, source_target_pairs={{0,16},{4,20},{8,24},{12,28},{16,0},{20,4},{24,8},{28,12},{1,17},{... | collective-permute-start | bytes 3538952 | tf_op jit(solution)/shard_map/ppermute | solution.py:189
  209.8 71.0 %collective-permute-start.21 = (bf16[1,448,1024]{2,1,0:T(8,128)(2,1)}, bf16[1,448,1024]{2,1,0:T(8,128)(2,1)}, u32[]{:S(2)}, u32[]{:S(2)}) collective-permute-start(bf16[1,448,1024]{2,1,0:T(8,128)(2,1)} %get-tuple-element.66), channel_id=1, source_target_pairs={{0,1},{1,0},{2,3},{3,2},{4,5},{5,4},{6,7},{7,6},{8,9},{9,8},{10,11... | collective-permute-start | bytes 2752520 | tf_op jit(solution)/shard_map/ppermute | solution.py:192
  211.4 87.3 %collective-permute-start.34 = (bf16[768,1024]{1,0:T(8,128)(2,1)}, bf16[768,1024]{1,0:T(8,128)(2,1)S(1)}, u32[]{:S(2)}, u32[]{:S(2)}) collective-permute-start(bf16[768,1024]{1,0:T(8,128)(2,1)} %slice.44.refs_8_), channel_id=1, source_target_pairs={{0,8},{4,12},{8,0},{12,4},{16,24},{20,28},{24,16},{28,20},{1,9},{5... | collective-permute-start | bytes 4718600 | tf_op jit(solution)/shard_map/ppermute | solution.py:189
  265.8 28.8 %collective-permute-start.23 = (bf16[1,448,1024]{2,1,0:T(8,128)(2,1)}, bf16[1,448,1024]{2,1,0:T(8,128)(2,1)S(1)}, u32[]{:S(2)}, u32[]{:S(2)}) collective-permute-start(bf16[1,448,1024]{2,1,0:T(8,128)(2,1)} %get-tuple-element.67), channel_id=1, source_target_pairs={{0,3},{1,2},{2,1},{3,0},{4,7},{5,6},{6,5},{7,4},{8,11},{9,10},{10,... | collective-permute-start | bytes 2752520 | tf_op jit(solution)/shard_map/ppermute | solution.py:192
  268.3 83.7 %collective-permute-start.5 = (bf16[1024,1024]{1,0:T(8,128)(2,1)}, bf16[1024,1024]{1,0:T(8,128)(2,1)}, u32[]{:S(2)}, u32[]{:S(2)}) collective-permute-start(bf16[1024,1024]{1,0:T(8,128)(2,1)} %get-tuple-element.24), channel_id=1, source_target_pairs={{0,16},{4,20},{8,24},{12,28},{16,0},{20,4},{24,8},{28,12},{1,17},{... | collective-permute-start | bytes 6291464 | tf_op jit(solution)/shard_map/ppermute | solution.py:189
  280.8 67.7 %collective-permute-start.9 = (bf16[768,1024]{1,0:T(8,128)(2,1)}, bf16[768,1024]{1,0:T(8,128)(2,1)}, u32[]{:S(2)}, u32[]{:S(2)}) collective-permute-start(bf16[768,1024]{1,0:T(8,128)(2,1)} %get-tuple-element.26), channel_id=1, source_target_pairs={{0,8},{4,12},{8,0},{12,4},{16,24},{20,28},{24,16},{28,20},{1,9},{5... | collective-permute-start | bytes 4718600 | tf_op jit(solution)/shard_map/ppermute | solution.py:189
  283.1 62.8 %collective-permute-start.22 = (bf16[1,448,1024]{2,1,0:T(8,128)(2,1)}, bf16[1,448,1024]{2,1,0:T(8,128)(2,1)}, u32[]{:S(2)}, u32[]{:S(2)}) collective-permute-start(bf16[1,448,1024]{2,1,0:T(8,128)(2,1)} %get-tuple-element.68), channel_id=1, source_target_pairs={{0,2},{1,3},{2,0},{3,1},{4,6},{5,7},{6,4},{7,5},{8,10},{9,11},{10,... | collective-permute-start | bytes 2752520 | tf_op jit(solution)/shard_map/ppermute | solution.py:192
  294.6 62.9 %collective-permute-start.33 = (bf16[768,1024]{1,0:T(8,128)(2,1)}, bf16[768,1024]{1,0:T(8,128)(2,1)}, u32[]{:S(2)}, u32[]{:S(2)}) collective-permute-start(bf16[768,1024]{1,0:T(8,128)(2,1)} %get-tuple-element.34), channel_id=1, source_target_pairs={{0,8},{4,12},{8,0},{12,4},{16,24},{20,28},{24,16},{28,20},{1,9},{5... | collective-permute-start | bytes 4718600 | tf_op jit(solution)/shard_map/ppermute | solution.py:189
  299.8 85.3 %collective-permute-start.28 = (bf16[1,448,1024]{2,1,0:T(8,128)(2,1)}, bf16[1,448,1024]{2,1,0:T(8,128)(2,1)}, u32[]{:S(2)}, u32[]{:S(2)}) collective-permute-start(bf16[1,448,1024]{2,1,0:T(8,128)(2,1)} %get-tuple-element.63), channel_id=1, source_target_pairs={{0,1},{1,0},{2,3},{3,2},{4,5},{5,4},{6,7},{7,6},{8,9},{9,8},{10,11... | collective-permute-start | bytes 2752520 | tf_op jit(solution)/shard_map/ppermute | solution.py:192
  348.5 39.3 %collective-permute-start.30 = (bf16[1,448,1024]{2,1,0:T(8,128)(2,1)}, bf16[1,448,1024]{2,1,0:T(8,128)(2,1)S(1)}, u32[]{:S(2)}, u32[]{:S(2)}) collective-permute-start(bf16[1,448,1024]{2,1,0:T(8,128)(2,1)} %get-tuple-element.64), channel_id=1, source_target_pairs={{0,3},{1,2},{2,1},{3,0},{4,7},{5,6},{6,5},{7,4},{8,11},{9,10},{10,... | collective-permute-start | bytes 2752520 | tf_op jit(solution)/shard_map/ppermute | solution.py:192
  352.0 74.2 %collective-permute-start.29 = (bf16[1,448,1024]{2,1,0:T(8,128)(2,1)S(1)}, bf16[1,448,1024]{2,1,0:T(8,128)(2,1)S(1)}, u32[]{:S(2)}, u32[]{:S(2)}) collective-permute-start(bf16[1,448,1024]{2,1,0:T(8,128)(2,1)S(1)} %copy-done.39), channel_id=1, source_target_pairs={{0,2},{1,3},{2,0},{3,1},{4,6},{5,7},{6,4},{7,5},{8,10},{9,11},{10,... | collective-permute-start | bytes 2752520 | tf_op jit(solution)/shard_map/ppermute | solution.py:192
  357.5 98.6 %collective-permute-start.10 = (f32[1792,512]{1,0:T(8,128)}, f32[1792,512]{1,0:T(8,128)}, u32[]{:S(2)}, u32[]{:S(2)}) collective-permute-start(f32[1792,512]{1,0:T(8,128)} %pad_maximum_fusion), channel_id=1, source_target_pairs={{0,4},{4,0},{8,12},{12,8},{16,20},{20,16},{24,28},{28,24},{1,5},{5... | collective-permute-start | bytes 11010056 | tf_op jit(solution)/shard_map/ppermute | solution.py:195
  372.5 73.2 %collective-permute-start.36 = (f32[384,1024]{1,0:T(8,128)}, f32[384,1024]{1,0:T(8,128)}, u32[]{:S(2)}, u32[]{:S(2)}) collective-permute-start(f32[384,1024]{1,0:T(8,128)} %get-tuple-element.76), channel_id=1, source_target_pairs={{0,4},{4,0},{8,12},{12,8},{16,20},{20,16},{24,28},{28,24},{1,5},{5... | collective-permute-start | bytes 4718600 | tf_op jit(solution)/shard_map/ppermute | solution.py:195
  385.1 46.2 %collective-permute-start.37 = (f32[384,768]{1,0:T(8,128)S(1)}, f32[384,768]{1,0:T(8,128)S(1)}, u32[]{:S(2)}, u32[]{:S(2)}) collective-permute-start(f32[384,768]{1,0:T(8,128)S(1)} %get-tuple-element.78), channel_id=1, source_target_pairs={{0,4},{4,0},{8,12},{12,8},{16,20},{20,16},{24,28},{28,24},{1,5},{5... | collective-permute-start | bytes 3538952 | tf_op jit(solution)/shard_map/ppermute | solution.py:195
  387.8 68.3 %collective-permute-start.24 = (bf16[4,448,512]{2,1,0:T(8,128)(2,1)}, bf16[4,448,512]{2,1,0:T(8,128)(2,1)}, u32[]{:S(2)}, u32[]{:S(2)}) collective-permute-start(bf16[4,448,512]{2,1,0:T(8,128)(2,1)} %pad_maximum_fusion.4), channel_id=1, source_target_pairs={{0,4},{4,0},{8,12},{12,8},{16,20},{20,16},{24,28},{28,24},{1,5},{5... | collective-permute-start | bytes 5505032 | tf_op jit(solution)/shard_map/ppermute | solution.py:195
  (49 other events, 654.0 us)
